TPU v7x, 32 devices: a whole 2x2x4 slice. The times are simulated.
32 devices in a mesh: grp: 2 (over x), seq: 16 (over z, y, core).
Axes of the slice: x: 2, y: 2, z: 4, core: 2. Of those that a mesh axis runs over, the one named last changes fastest.
Arguments:
- alignment: bfloat16 [64, 128, 768], P(('grp', 'seq')), parts along dimension 0, may hold values from -20 to 20
- protein_id: int32 [256], P('grp'), parts along dimension 0, may hold values from 0 to 3, never falling along the last dimension, each value on 1 to 64 neighbouring positions
- row_depth: int32 [8], P('grp'), parts along dimension 0, may hold values from 8 to 32, as said below
- row_gain: float32 [768], replicated, may hold values from 0.1 to 1.9
- row_query: bfloat16 [768, 768], replicated, may hold values from -40 to 40
- row_key: bfloat16 [768, 768], replicated, may hold values from -0.21875 to 0.21875
- row_value: bfloat16 [768, 768], replicated, may hold values from -0.21875 to 0.21875
- row_output: bfloat16 [768, 768], replicated, may hold values from -0.21875 to 0.21875
- column_gain: float32 [768], replicated, may hold values from 0.1 to 1.9
- column_query: bfloat16 [768, 768], replicated, may hold values from -40 to 40
- column_key: bfloat16 [768, 768], replicated, may hold values from -0.21875 to 0.21875
- column_value: bfloat16 [768, 768], replicated, may hold values from -0.21875 to 0.21875
- column_output: bfloat16 [768, 768], replicated, may hold values from -0.21875 to 0.21875
Outputs:
- layer_out: bfloat16 [64, 128, 768], P(('grp', 'seq')), parts along dimension 0
There are 2 independent parts, one for each index of `grp`. A program takes and returns all parts, laid end to end along the dimension named above; an argument that names none is the same for every part. Nothing has to cross between parts.
Inputs may be any that keep to these rules, and one draw needn't show every extreme that they name: `row_depth`: row 0 is real for every protein; one protein of each pack has all 32 rows real. `protein_id`: proteins occupy contiguous column ranges in order, each 1 to 64 columns.
All inputs are finite; a program needn't handle non-finite values.
Results may differ from a plain program's by a relative error of at most 0.011.
Values may be sent and summed in bfloat16 or wider, within the bound.
No kernel may reach another device: no remote copies, remote signals or barrier semaphores. Data moves between devices by JAX's collectives and lax.ppermute only.
A program may use at most 64 MiB of HBM per device.

v0:
```python
import math
import jax
import jax.numpy as jnp
from jax import lax
from jax.sharding import PartitionSpec as P

H = 12


def layer_norm(values, gain):
    full = values.astype(jnp.float32)
    middle = jnp.mean(full, axis=-1, keepdims=True)
    spread = jnp.mean((full - middle) ** 2, axis=-1, keepdims=True)
    return ((full - middle) * lax.rsqrt(spread + 1e-05) * gain).astype(jnp.bfloat16)


def project(normed, weight):
    shape = normed.shape
    flattened = normed.reshape(-1, shape[-1])
    return (
        jnp.dot(flattened, weight, preferred_element_type=jnp.float32)
        .astype(jnp.bfloat16)
        .reshape(shape[:-1] + (weight.shape[1],))
    )


def column_depth(protein_id, row_depth):
    onehot = protein_id[:, None] == jnp.arange(row_depth.shape[0], dtype=jnp.int32)[None, :]
    return jnp.sum(jnp.where(onehot, row_depth[None, :], 0), axis=1)


def per_device(
    alignment,
    protein_id,
    row_depth,
    row_gain,
    row_query,
    row_key,
    row_value,
    row_output,
    column_gain,
    column_query,
    column_key,
    column_value,
    column_output,
):
    rows_dev, columns, width = alignment.shape
    devices = lax.axis_size("seq")
    position = lax.axis_index("seq")
    total_rows = rows_dev * devices
    head_count = H
    head_size = width // head_count
    tile_cols = columns // devices
    depth_col = column_depth(protein_id, row_depth)
    row_ids = position * rows_dev + jnp.arange(rows_dev, dtype=jnp.int32)
    valid = row_ids[:, None] < depth_col[None, :]
    mask_bf = valid.astype(jnp.bfloat16)[:, :, None]
    normed_row = layer_norm(alignment, row_gain)
    query_a = (project(normed_row, row_query) * mask_bf).reshape(
        rows_dev, columns, head_count, head_size
    )
    key_a = (project(normed_row, row_key) * mask_bf).reshape(
        rows_dev, columns, head_count, head_size
    )
    value_a = project(normed_row, row_value).reshape(rows_dev, columns, head_count, head_size)
    scale = 1.0 / (math.sqrt(head_size) * math.sqrt(total_rows))
    tied = (
        lax.psum_scatter(
            jnp.einsum("rihe,rjhe->ihj", query_a, key_a, preferred_element_type=jnp.float32),
            "seq",
            scatter_dimension=0,
            tiled=True,
        )
        * scale
    )
    prot_query = lax.dynamic_slice_in_dim(protein_id, position * tile_cols, tile_cols, 0)
    same_prot = prot_query[:, None, None] == protein_id[None, None, :]
    tied = jnp.where(same_prot, tied, -1000000000.0)
    row_weights = jax.nn.softmax(tied, axis=-1).astype(jnp.bfloat16)
    row_mixed = (
        jnp.einsum(
            "ihj,rjhe->rihe",
            lax.all_gather(row_weights, "seq", axis=0, tiled=True),
            value_a,
            preferred_element_type=jnp.float32,
        )
        .astype(jnp.bfloat16)
        .reshape(rows_dev, columns, width)
    )
    after_row = (
        alignment.astype(jnp.float32)
        + jnp.dot(
            row_mixed.reshape(-1, width), row_output, preferred_element_type=jnp.float32
        ).reshape(rows_dev, columns, width)
    ).astype(jnp.bfloat16)
    normed_col = layer_norm(after_row, column_gain)
    moved = lax.all_to_all(normed_col, "seq", split_axis=1, concat_axis=0, tiled=True)
    query_b = project(moved, column_query)
    key_b = project(moved, column_key)
    value_b = project(moved, column_value)
    query_b = query_b.reshape(total_rows, tile_cols, head_count, head_size)
    key_b = key_b.reshape(total_rows, tile_cols, head_count, head_size)
    value_b = value_b.reshape(total_rows, tile_cols, head_count, head_size)
    depth_tile = lax.dynamic_slice_in_dim(depth_col, position * tile_cols, tile_cols, 0)
    key_valid = jnp.arange(total_rows, dtype=jnp.int32)[None, :] < depth_tile[:, None]
    col_scores = jnp.einsum(
        "rche,sche->chrs", query_b, key_b, preferred_element_type=jnp.float32
    ) / math.sqrt(head_size)
    col_scores = jnp.where(key_valid[:, None, None, :], col_scores, -1000000000.0)
    col_weights = jax.nn.softmax(col_scores, axis=-1).astype(jnp.bfloat16)
    col_mixed = jnp.einsum(
        "chrs,sche->rche", col_weights, value_b, preferred_element_type=jnp.float32
    ).astype(jnp.bfloat16)
    col_mixed = col_mixed.reshape(total_rows, tile_cols, width)
    returned = lax.all_to_all(col_mixed, "seq", split_axis=0, concat_axis=1, tiled=True)
    layer_out = after_row.astype(jnp.float32) + jnp.dot(
        returned.reshape(-1, width), column_output, preferred_element_type=jnp.float32
    ).reshape(rows_dev, columns, width)
    return layer_out.astype(jnp.bfloat16)


def solution(mesh):
    return jax.shard_map(
        per_device,
        mesh=mesh,
        in_specs=(
            P(("grp", "seq"), None, None),
            P("grp"),
            P("grp"),
            P(),
            P(),
            P(),
            P(),
            P(),
            P(),
            P(),
            P(),
            P(),
            P(),
        ),
        out_specs=P(("grp", "seq"), None, None),
        check_vma=False,
    )
```

profile of v0, /device:TPU:0, one launch (start us, length us, event | category | flops | bytes accessed | tf_op | source)
XLA Modules:
  0.0 158.1 jit_solution(10954076205752719301)
XLA Ops:
  6.5 1.3 convert_reduce_fusion
  7.8 1.2 fusion.15
  9.1 1.2 fusion.17
  10.3 0.5 convolution_convert_fusion.5
  10.8 0.2 copy.75
  11.0 0.1 reshape.141
  11.1 1.7 %convolution_convert_fusion.4 = bf16[256,768]{1,0:T(8,128)(2,1)S(1)} fusion(bf16[256,768]{1,0:T(8,128)(2,1)S(1)} %bitcast.61, bf16[768,768]{1,0:T(8,128)(2,1)} %param.17), kind=kOutput, calls=%fused_computation.17 | convolution fusion | flops 302186496 | bytes 1966080 | tf_op jit(solution)/shard_map/dot_general | solution.py:21
  12.9 0.2 copy.76
  13.0 0.1 reshape.142
  13.2 0.3 copy-done.6
  13.5 0.0 copy-done.7
  13.5 0.1 select_reduce_fusion
  13.6 0.1 compare_convert_fusion
  13.7 0.1 broadcast_multiply_fusion.1
  13.7 0.3 convolution_bitcast_fusion
  14.1 0.0 copy-start.3
  14.1 1.4 copy.79
  15.5 0.0 reduce-scatter.2.cloned.1.call-update
  15.5 0.1 dynamic_slice.6
  15.6 0.5 convolution_convert_fusion.6
  16.1 0.2 copy.74
  16.2 0.1 reshape_reshape.13
  16.3 0.1 broadcast_compare_fusion
  16.4 59.4 %reduce-scatter.2.cloned.1.call-done = f32[8,12,128]{2,1,0:T(8,128)} async-done(((f32[128,12,128]{2,1,0:T(8,128)}), f32[8,12,128]{2,1,0:T(8,128)}) %reduce-scatter.2.cloned.1.call-update) | async-done | bytes 49168 | tf_op jit(solution)/shard_map/reduce_scatter | solution.py:68
  75.8 1.0 fusion.38
  76.8 0.1 divide_convert_fusion.2
  76.9 20.5 %all_gather.3 = bf16[128,12,128]{2,0,1:T(8,128)(2,1)S(1)} all-gather(bf16[8,12,128]{2,0,1:T(8,128)(2,1)S(1)} %copy.80), channel_id=1, replica_groups=mesh['grp'=2,'seq'=16] {'seq'}, dimensions={0}, use_global_device_ids=true | all-gather | bytes 417792 | tf_op jit(solution)/shard_map/all_gather | solution.py:83
  97.5 0.4 fusion.8
  97.9 0.6 fusion.39
  98.5 0.2 multiply_reduce_fusion
  98.8 0.2 multiply_convert_fusion
  99.0 1.2 copy.84
  100.1 3.6 %all-to-all-start = ((bf16[2,128,768]{2,0,1:T(2,128)(2,1)}), bf16[2,128,768]{2,0,1:T(2,128)(2,1)S(1)}, u32[]{:S(2)}, u32[]{:S(2)}) async-start(bf16[2,128,768]{2,0,1:T(2,128)(2,1)} %copy.84), calls=%async_computation.1 | async-start | bytes 786432 | tf_op jit(solution)/shard_map/all_to_all | solution.py:97
  103.7 0.1 dynamic_slice.7
  103.7 0.1 iota_compare_fusion
  103.8 12.0 %all-to-all-done = bf16[2,128,768]{2,0,1:T(2,128)(2,1)S(1)} async-done(((bf16[2,128,768]{2,0,1:T(2,128)(2,1)}), bf16[2,128,768]{2,0,1:T(2,128)(2,1)S(1)}, u32[]{:S(2)}, u32[]{:S(2)}) %all-to-all-start) | async-done | bytes 393248 | tf_op jit(solution)/shard_map/all_to_all | solution.py:97
  115.9 1.7 %convolution_convert_fusion.2 = bf16[256,768]{1,0:T(8,128)(2,1)S(1)} fusion(bf16[256,768]{1,0:T(8,128)(2,1)S(1)} %bitcast.63, bf16[768,768]{1,0:T(8,128)(2,1)} %param.22), kind=kOutput, calls=%fused_computation.15 | convolution fusion | flops 302186496 | bytes 1966080 | tf_op jit(solution)/shard_map/dot_general | solution.py:21
  117.7 1.6 %reshape_reshape.15 = bf16[32,8,12,64]{3,2,1,0:T(8,128)(2,1)} reshape(bf16[256,768]{1,0:T(8,128)(2,1)S(1)} %convolution_convert_fusion.2) | data formatting | bytes 786432 | tf_op jit(solution)/shard_map/reshape;reshape | solution.py:101
  119.3 1.7 %convolution_convert_fusion.1 = bf16[256,768]{1,0:T(8,128)(2,1)S(1)} fusion(bf16[256,768]{1,0:T(8,128)(2,1)S(1)} %bitcast.64, bf16[768,768]{1,0:T(8,128)(2,1)} %param.23), kind=kOutput, calls=%fused_computation.14 | convolution fusion | flops 302186496 | bytes 1966080 | tf_op jit(solution)/shard_map/dot_general | solution.py:21
  121.0 1.6 reshape_reshape.16
  122.6 1.7 %convolution_convert_fusion.3 = bf16[256,768]{1,0:T(8,128)(2,1)S(1)} fusion(bf16[256,768]{1,0:T(8,128)(2,1)S(1)} %bitcast.65, bf16[768,768]{1,0:T(8,128)(2,1)} %param.24), kind=kOutput, calls=%fused_computation.16 | convolution fusion | flops 302186496 | bytes 1966080 | tf_op jit(solution)/shard_map/dot_general | solution.py:21
  124.3 1.6 reshape_reshape.14
  125.9 4.2 %fusion.40 = (f32[8,12,32]{2,1,0:T(8,128)S(1)}, f32[8,12,32,32]{2,3,1,0:T(8,128)}) fusion(bf16[32,8,12,64]{3,2,1,0:T(8,128)(2,1)} %reshape_reshape.16, bf16[32,8,12,64]{3,2,1,0:T(8,128)(2,1)} %reshape_reshape.15, pred[8,32]{1,0:T(8,128)(4,1)S(1)} %iota_compare_fusion), kind=kOutput, calls=%fused_computation.68 | convolution fusion | flops 12976159 | bytes 1192192 | tf_op jit(solution)/shard_map/sub | solution.py:110
  130.1 2.1 %fusion.4 = bf16[32,8,12,64]{3,0,2,1:T(8,128)(2,1)S(1)} fusion(f32[8,12,32,32]{2,3,1,0:T(8,128)} %get-tuple-element.12, bf16[32,8,12,64]{3,2,1,0:T(8,128)(2,1)S(1)} %copy-done.4, f32[8,12,32]{2,1,0:T(8,128)S(1)} %get-tuple-element.11), kind=kOutput, calls=%fused_computation.7 | convolution fusion | flops 12976128 | bytes 1191936 | tf_op jit(solution)/shard_map/chrs,sche->rche/dot_general | solution.py:111
  132.3 0.3 copy.91
  132.6 0.6 reshape.144
  133.3 15.5 %all_to_all.30 = bf16[32,8,768]{2,1,0:T(8,128)(2,1)S(1)} all-to-all(bf16[32,8,768]{2,1,0:T(8,128)(2,1)S(1)} %reshape.144), channel_id=1, replica_groups=mesh['grp'=2,'seq'=16] {'seq'}, dimensions={0} | all-to-all | bytes 786432 | tf_op jit(solution)/shard_map/all_to_all | solution.py:115
  148.7 2.5 %fusion.7 = bf16[2,128,768]{2,1,0:T(8,128)(2,1)} fusion(f32[2,128,768]{2,1,0:T(8,128)S(1)} %get-tuple-element.10, bf16[768,768]{1,0:T(8,128)(2,1)} %param.25, bf16[2,16,8,768]{3,2,0,1:T(8,128)(2,1)S(1)} %bitcast.72), kind=kOutput, calls=%fused_computation.13 | convolution fusion | flops 302383104 | bytes 2752512 | tf_op jit(solution)/shard_map/dot_general | solution.py:116
  (24 shorter events, 0.2 us)
Async XLA Ops:
  6.5 91.4 %copy-start = (bf16[768,768]{1,0:T(8,128)(2,1)S(1)}, bf16[768,768]{1,0:T(8,128)(2,1)}, u32[]{:S(2)}) copy-start(bf16[768,768]{1,0:T(8,128)(2,1)} %param.20) | copy-start | bytes 3538948
  6.5 3.8 %copy-start.2 = (bf16[768,768]{1,0:T(8,128)(2,1)S(1)}, bf16[768,768]{1,0:T(8,128)(2,1)}, u32[]{:S(2)}) copy-start(bf16[768,768]{1,0:T(8,128)(2,1)} %param.18) | copy-start | bytes 3538948
  6.5 69.2 %reduce-scatter.2.cloned.1.call-start = ((), (), s32[]{:S(2)}) async-start(), calls=%async_computation.3 | async-start | bytes 1114112 | tf_op jit(solution)/shard_map/reduce_scatter | solution.py:68
  12.8 0.7 copy-start.6
  12.8 0.7 copy-start.7
  14.1 1.5 copy-start.3
  76.9 21.0 %copy-start.1 = (bf16[2,128,768]{2,1,0:T(8,128)(2,1)S(1)}, bf16[2,128,768]{2,1,0:T(8,128)(2,1)}, u32[]{:S(2)}) copy-start(bf16[2,128,768]{2,1,0:T(8,128)(2,1)} %param.13) | copy-start | bytes 1179652
  97.9 0.8 copy-start.5
  100.1 15.7 %all-to-all-start = ((bf16[2,128,768]{2,0,1:T(2,128)(2,1)}), bf16[2,128,768]{2,0,1:T(2,128)(2,1)S(1)}, u32[]{:S(2)}, u32[]{:S(2)}) async-start(bf16[2,128,768]{2,0,1:T(2,128)(2,1)} %copy.84), calls=%async_computation.1 | async-start | bytes 786432 | tf_op jit(solution)/shard_map/all_to_all | solution.py:97
  125.9 4.2 %copy-start.4 = (bf16[32,8,12,64]{3,2,1,0:T(8,128)(2,1)S(1)}, bf16[32,8,12,64]{3,2,1,0:T(8,128)(2,1)}, u32[]{:S(2)}) copy-start(bf16[32,8,12,64]{3,2,1,0:T(8,128)(2,1)} %reshape_reshape.14) | copy-start | bytes 1179652
Sparse Core Ops, SparseCore 0:
  15.6 60.1 reduce-scatter.1
where the time goes:
time: 159 us; the launch traced here: 158 us
  waiting for transfers between devices  71.4 us (45%)
  blocking collectives  36 us (23%)
  matrix products  18.1 us (11%)
  between operations  13.7 us (9%)
  local copies, waits for them, and re-layouts  9.7 us (6%)
  other arithmetic  5.64 us (4%)
  starting transfers between devices  3.56 us (2%)
    reduce_scatter x1, waiting for transfers between devices, per_device(): lax.psum_scatter(jnp.einsum('rihe,rjhe->ihj', query_a, key_a, preferred_e...  59.4 us
    all_gather x1, blocking collectives, per_device(): lax.all_gather(row_weights, 'seq', axis=0, tiled=True)  20.5 us
    all_to_all x1, blocking collectives, per_device(): lax.all_to_all(col_mixed, 'seq', split_axis=0, concat_axis=1, tiled=True)  15.5 us
    all_to_all x1, waiting for transfers between devices, per_device(): lax.all_to_all(normed_col, 'seq', split_axis=1, concat_axis=0, tiled=True)  12 us
    dot_general x6, matrix products, project(): jnp.dot(flattened, weight, preferred_element_type=jnp.float32)  7.94 us
    sub x1, matrix products, per_device(): col_weights = jax.nn.softmax(col_scores, axis=-1).astype(jnp.bfloat16)  4.24 us
    all_to_all x1, starting transfers between devices, per_device(): lax.all_to_all(normed_col, 'seq', split_axis=1, concat_axis=0, tiled=True)  3.55 us
  transfers between devices with their start and end apart: 2, of which 2 were waited for; matrix products, arithmetic and copies ran while one was open for 1% of the time, Pallas kernels for 0%

commit v1 on v0

--- a/solution.py
+++ b/solution.py
@@ -112,7 +112,10 @@
         "chrs,sche->rche", col_weights, value_b, preferred_element_type=jnp.float32
     ).astype(jnp.bfloat16)
     col_mixed = col_mixed.reshape(total_rows, tile_cols, width)
-    returned = lax.all_to_all(col_mixed, "seq", split_axis=0, concat_axis=1, tiled=True)
+    returned = jnp.concatenate(
+        lax.all_to_all(jnp.stack(jnp.split(col_mixed, lax.axis_size("seq"), axis=0)), "seq", 0, 0),
+        axis=1,
+    )
     layer_out = after_row.astype(jnp.float32) + jnp.dot(
         returned.reshape(-1, width), column_output, preferred_element_type=jnp.float32
     ).reshape(rows_dev, columns, width)

time: 159 us -> 190 us (1.19)
  local copies, waits for them, and re-layouts: 9.7 us -> 42.3 us
    another operation x0 -> x17, local copies, waits for them, and re-layouts: none -> 14.8 us  [per_device(): jnp.stack(jnp.split(col_mixed, lax.axis_size('seq'), axis=0))]
    unnamed x17 -> x34, local copies, waits for them, and re-layouts: 0.4 us -> 11.7 us
    split x0 -> x17, local copies, waits for them, and re-layouts: none -> 7.45 us  [per_device(): jnp.split(col_mixed, lax.axis_size('seq'), axis=0)]
where the time goes in v1:
time: 190 us; the launch traced here: 188 us
  waiting for transfers between devices  69.9 us (37%)
  local copies, waits for them, and re-layouts  42.3 us (22%)
  blocking collectives  36 us (19%)
  matrix products  16.8 us (9%)
  between operations  13.7 us (7%)
  other arithmetic  5.64 us (3%)
  starting transfers between devices  3.74 us (2%)
    reduce_scatter x1, waiting for transfers between devices, per_device(): lax.psum_scatter(jnp.einsum('rihe,rjhe->ihj', query_a, key_a, preferred_e...  58.1 us
    all_gather x1, blocking collectives, per_device(): lax.all_gather(row_weights, 'seq', axis=0, tiled=True)  20.5 us
    all_to_all x1, blocking collectives, per_device(): lax.all_to_all(jnp.stack(jnp.split(col_mixed, lax.axis_size('seq'), axis=...  15.5 us
    another operation x17, local copies, waits for them, and re-layouts, per_device(): jnp.stack(jnp.split(col_mixed, lax.axis_size('seq'), axis=0))  14.8 us
    all_to_all x1, waiting for transfers between devices, per_device(): lax.all_to_all(normed_col, 'seq', split_axis=1, concat_axis=0, tiled=True)  11.8 us
    unnamed x34, local copies, waits for them, and re-layouts  11.7 us
    dot_general x6, matrix products, project(): jnp.dot(flattened, weight, preferred_element_type=jnp.float32)  7.94 us
    split x17, local copies, waits for them, and re-layouts, per_device(): jnp.split(col_mixed, lax.axis_size('seq'), axis=0)  7.45 us
  transfers between devices with their start and end apart: 2, of which 2 were waited for; matrix products, arithmetic and copies ran while one was open for 1% of the time, Pallas kernels for 0%

profile of v1, /device:TPU:0, one launch (start us, length us, event | category | flops | bytes accessed | tf_op | source)
XLA Modules:
  0.0 188.2 jit_solution(1822983468582941143)
XLA Ops:
  6.5 1.3 convert_reduce_fusion
  7.8 1.2 fusion.15
  9.1 1.2 fusion.17
  11.1 1.0 copy-done.3
  13.8 1.4 copy.124
  15.3 1.7 convolution_convert_fusion.6
  17.4 58.1 %reduce-scatter.2.cloned.1.call-done = f32[8,12,128]{2,1,0:T(8,128)} async-done(((f32[128,12,128]{2,1,0:T(8,128)}), f32[8,12,128]{2,1,0:T(8,128)}) %reduce-scatter.2.cloned.1.call-update) | async-done | bytes 49168 | tf_op jit(solution)/shard_map/reduce_scatter | solution.py:68
  75.5 1.0 fusion.39
  76.6 20.5 %all_gather.3 = bf16[128,12,128]{2,0,1:T(8,128)(2,1)S(1)} all-gather(bf16[8,12,128]{2,0,1:T(8,128)(2,1)S(1)} %copy.125), channel_id=1, replica_groups=mesh['grp'=2,'seq'=16] {'seq'}, dimensions={0}, use_global_device_ids=true | all-gather | bytes 417792 | tf_op jit(solution)/shard_map/all_gather | solution.py:83
  98.7 1.2 copy.129
  99.8 3.7 %all-to-all-start = ((bf16[2,128,768]{2,0,1:T(2,128)(2,1)}), bf16[2,128,768]{2,0,1:T(2,128)(2,1)S(1)}, u32[]{:S(2)}, u32[]{:S(2)}) async-start(bf16[2,128,768]{2,0,1:T(2,128)(2,1)} %copy.129), calls=%async_computation.1 | async-start | bytes 786432 | tf_op jit(solution)/shard_map/all_to_all | solution.py:97
  103.7 11.8 %all-to-all-done = bf16[2,128,768]{2,0,1:T(2,128)(2,1)S(1)} async-done(((bf16[2,128,768]{2,0,1:T(2,128)(2,1)}), bf16[2,128,768]{2,0,1:T(2,128)(2,1)S(1)}, u32[]{:S(2)}, u32[]{:S(2)}) %all-to-all-start) | async-done | bytes 393248 | tf_op jit(solution)/shard_map/all_to_all | solution.py:97
  115.6 1.7 convolution_convert_fusion.2
  117.4 1.6 reshape_reshape.16
  119.0 1.7 convolution_convert_fusion.1
  120.7 1.6 reshape_reshape.17
  122.3 1.7 convolution_convert_fusion.3
  124.0 1.6 reshape_reshape.15
  125.6 4.2 %fusion.41 = (f32[8,12,32]{2,1,0:T(8,128)S(1)}, f32[8,12,32,32]{2,3,1,0:T(8,128)}) fusion(bf16[32,8,12,64]{3,2,1,0:T(8,128)(2,1)} %reshape_reshape.17, bf16[32,8,12,64]{3,2,1,0:T(8,128)(2,1)} %reshape_reshape.16, pred[8,32]{1,0:T(8,128)(4,1)S(1)} %iota_compare_fusion), kind=kOutput, calls=%fused_computation.85 | convolution fusion | flops 12976159 | bytes 1192192 | tf_op jit(solution)/shard_map/sub | solution.py:110
  129.8 2.1 %fusion.4 = bf16[32,8,12,64]{3,0,2,1:T(8,128)(2,1)S(1)} fusion(f32[8,12,32,32]{2,3,1,0:T(8,128)} %get-tuple-element.28, bf16[32,8,12,64]{3,2,1,0:T(8,128)(2,1)S(1)} %copy-done.5, f32[8,12,32]{2,1,0:T(8,128)S(1)} %get-tuple-element.27), kind=kOutput, calls=%fused_computation.7 | convolution fusion | flops 12976128 | bytes 1191936 | tf_op jit(solution)/shard_map/chrs,sche->rche/dot_general | solution.py:111
  132.0 1.5 fusion.38
  134.3 0.7 stack.53
  136.5 0.7 stack.56
  141.5 1.5 copy.148
  143.1 1.5 stack.63
  144.6 1.4 copy.149
  146.1 1.5 stack.64
  147.6 1.4 copy.150
  149.0 1.6 stack.65
  150.6 1.4 copy.151
  152.0 1.5 stack.66
  153.6 0.7 constant_dynamic-update-slice_fusion.14
  154.3 0.7 constant_dynamic-update-slice_fusion.13
  155.1 0.7 constant_dynamic-update-slice_fusion.12
  155.8 0.7 constant_dynamic-update-slice_fusion.11
  156.5 0.7 constant_dynamic-update-slice_fusion.10
  157.3 0.7 constant_dynamic-update-slice_fusion.9
  158.0 0.7 constant_dynamic-update-slice_fusion.8
  158.7 0.7 constant_dynamic-update-slice_fusion.7
  159.5 0.7 constant_dynamic-update-slice_fusion.6
  160.2 0.7 constant_dynamic-update-slice_fusion.5
  161.0 0.7 constant_dynamic-update-slice_fusion.4
  161.7 0.7 constant_dynamic-update-slice_fusion.3
  162.4 0.7 constant_dynamic-update-slice_fusion.2
  163.2 0.7 constant_dynamic-update-slice_fusion.1
  163.9 0.7 constant_dynamic-update-slice_fusion
  164.7 15.5 %all_to_all.20 = bf16[16,2,8,768]{3,2,1,0:T(8,128)(2,1)S(1)} all-to-all(bf16[16,2,8,768]{3,2,1,0:T(8,128)(2,1)S(1)} %constant_dynamic-update-slice_fusion), channel_id=1, replica_groups=mesh['grp'=2,'seq'=16] {'seq'}, dimensions={0} | all-to-all | bytes 786432 | tf_op jit(solution)/shard_map/all_to_all | solution.py:116
  180.1 1.2 fusion.7
  (73 shorter events, 11.2 us)
Async XLA Ops:
  6.5 91.1 %copy-start = (bf16[768,768]{1,0:T(8,128)(2,1)S(1)}, bf16[768,768]{1,0:T(8,128)(2,1)}, u32[]{:S(2)}) copy-start(bf16[768,768]{1,0:T(8,128)(2,1)} %param.20) | copy-start | bytes 3538948
  6.5 3.8 %copy-start.2 = (bf16[768,768]{1,0:T(8,128)(2,1)S(1)}, bf16[768,768]{1,0:T(8,128)(2,1)}, u32[]{:S(2)}) copy-start(bf16[768,768]{1,0:T(8,128)(2,1)} %param.18) | copy-start | bytes 3538948
  6.5 68.9 %reduce-scatter.2.cloned.1.call-start = ((), (), s32[]{:S(2)}) async-start(), calls=%async_computation.3 | async-start | bytes 1114112 | tf_op jit(solution)/shard_map/reduce_scatter | solution.py:68
  10.8 1.3 copy-start.3
  12.6 0.7 copy-start.7
  12.6 0.7 copy-start.8
  76.6 21.0 %copy-start.1 = (bf16[2,128,768]{2,1,0:T(8,128)(2,1)S(1)}, bf16[2,128,768]{2,1,0:T(8,128)(2,1)}, u32[]{:S(2)}) copy-start(bf16[2,128,768]{2,1,0:T(8,128)(2,1)} %param.13) | copy-start | bytes 1179652
  97.6 0.8 copy-start.6
  99.8 15.7 %all-to-all-start = ((bf16[2,128,768]{2,0,1:T(2,128)(2,1)}), bf16[2,128,768]{2,0,1:T(2,128)(2,1)S(1)}, u32[]{:S(2)}, u32[]{:S(2)}) async-start(bf16[2,128,768]{2,0,1:T(2,128)(2,1)} %copy.129), calls=%async_computation.1 | async-start | bytes 786432 | tf_op jit(solution)/shard_map/all_to_all | solution.py:97
  125.6 4.2 %copy-start.5 = (bf16[32,8,12,64]{3,2,1,0:T(8,128)(2,1)S(1)}, bf16[32,8,12,64]{3,2,1,0:T(8,128)(2,1)}, u32[]{:S(2)}) copy-start(bf16[32,8,12,64]{3,2,1,0:T(8,128)(2,1)} %reshape_reshape.15) | copy-start | bytes 1179652
  141.5 38.6 %copy-start.4 = (bf16[768,768]{1,0:T(8,128)(2,1)S(1)}, bf16[768,768]{1,0:T(8,128)(2,1)}, u32[]{:S(2)}) copy-start(bf16[768,768]{1,0:T(8,128)(2,1)} %param.25) | copy-start | bytes 3538948
Sparse Core Ops, SparseCore 0:
  15.3 60.1 reduce-scatter.1
